TPU v7x, 32 devices: a whole 2x2x4 slice. The times are simulated.
32 devices in a mesh: grp: 4 (over z), grid: 8 (over y, x, core).
Axes of the slice: x: 2, y: 2, z: 4, core: 2. Of those that a mesh axis runs over, the one named last changes fastest.
Arguments:
- vectors: float32 [4, 3, 2, 32, 256, 256], P('grp', None, None, 'grid'), may hold values from -6 to 6
- potential: float32 [32, 256, 256], P('grid'), may hold values from 0.1 to 2
- added_field: float32 [4, 32, 256, 256], P('grp', 'grid'), may hold values from -3 to 3
- qp_states: bfloat16 [32, 32, 256, 256], P(None, 'grid'), may hold values from -0.00390625 to 0.00390625
Outputs:
- elements: float32 [4, 32, 6], P('grp', 'grid')
All inputs are finite; a program needn't handle non-finite values.
Results may differ from a plain program's by a relative error of at most 0.0033.
Values sent between devices are 32-bit elements; how exact they have to be, the bound alone decides.
No kernel may reach another device: no remote copies, remote signals or barrier semaphores. Data moves between devices by JAX's collectives and lax.ppermute only.
A program may use at most 256 MiB of HBM per device.

v0:
```python
import jax
import jax.numpy as jnp
from jax import lax
from jax.sharding import PartitionSpec as P

ORDER = 4
time_step = 0.2
four_pi = 12.566370614359172


def padded_2(block, sides, width):
    for axis, dim in sides:
        count = lax.axis_size(axis)
        forward = [(i, i + 1) for i in range(count - 1)]
        backward = [(target, source) for source, target in forward]
        low = lax.ppermute(
            lax.slice_in_dim(block, block.shape[dim] - width, None, axis=dim), axis, forward
        )
        high = lax.ppermute(lax.slice_in_dim(block, 0, width, axis=dim), axis, backward)
        block = jnp.concatenate([low, block, high], axis=dim)
    return block


def shifted(array, axis, by):
    peers = lax.axis_size(axis)
    pairs = [(i, i + by) for i in range(peers) if 0 <= i + by < peers]
    return lax.ppermute(array, axis, pairs)


def sine_table(length):
    indices = jnp.arange(length, dtype=jnp.int32) + 1
    products = indices[:, None] * indices[None, :] % (2 * (length + 1))
    return jnp.sqrt(2.0 / (length + 1)) * jnp.sin(
        jnp.pi * products.astype(jnp.float32) / (length + 1)
    )


def eigenvalues(length):
    indices = jnp.arange(length, dtype=jnp.int32) + 1
    return 2.0 - 2.0 * jnp.cos(jnp.pi * indices.astype(jnp.float32) / (length + 1))


def laplace_inner(field):
    centre = field[..., 1:-1, :, :]
    result = field[..., 2:, :, :] + field[..., :-2, :, :]
    widths = [(0, 0)] * (centre.ndim - 2)
    along_y = jnp.pad(centre, widths + [(1, 1), (0, 0)])
    result = result + along_y[..., 2:, :] + along_y[..., :-2, :]
    along_z = jnp.pad(centre, widths + [(0, 0), (1, 1)])
    result = result + along_z[..., 2:] + along_z[..., :-2]
    return result - 6.0 * centre


def taylor_term(applied, power):
    factor = time_step / power
    return jnp.stack([factor * applied[:, :, 1], -factor * applied[:, :, 0]], axis=2)


def poisson_block(density):
    highest = lax.Precision.HIGHEST
    planes = density.shape[0]
    size_y = density.shape[1]
    size_z = density.shape[2]
    full_x = planes * lax.axis_size("grid")
    table_x = sine_table(full_x)
    table_y = sine_table(size_y)
    table_z = sine_table(size_z)
    field = jnp.einsum("xyz,zl->xyl", density, table_z, precision=highest)
    field = jnp.einsum("xyl,yk->xkl", field, table_y, precision=highest)
    columns = lax.all_to_all(field, "grid", split_axis=1, concat_axis=0, tiled=True)
    row_count = columns.shape[1]
    own_rows = lax.dynamic_slice_in_dim(
        eigenvalues(size_y), lax.axis_index("grid") * row_count, row_count
    )
    field = jnp.einsum("xkl,xm->mkl", columns, table_x, precision=highest)
    spectrum = (
        eigenvalues(full_x)[:, None, None]
        + own_rows[None, :, None]
        + eigenvalues(size_z)[None, None, :]
    )
    field = field * (four_pi / spectrum)
    field = jnp.einsum("mkl,mx->xkl", field, table_x, precision=highest)
    returned = lax.all_to_all(field, "grid", split_axis=0, concat_axis=1, tiled=True)
    field = jnp.einsum("xkl,ky->xyl", returned, table_y, precision=highest)
    return jnp.einsum("xyl,lz->xyz", field, table_z, precision=highest)


def on_device(vectors, potential, added_field, qp_states):
    initial = vectors[0]
    state = jnp.stack([initial, initial])
    fields = jnp.stack([potential, potential + added_field[0]])
    summed = state
    current = state
    for power in range(1, ORDER + 1):
        padded = padded_2(current, (("grid", 3),), 1)
        applied = -0.5 * laplace_inner(padded) + fields[:, None, None] * current
        current = taylor_term(applied, power)
        summed = summed + current
    density = jnp.sum(summed[1] * summed[1] - summed[0] * summed[0], axis=(0, 1))
    induced = poisson_block(density)
    received = shifted(induced, "grp", lax.axis_size("grp") // 2)
    weighted = ((received + added_field[0]) * summed[1]).astype(jnp.bfloat16)
    flat_weighted = weighted.reshape(weighted.shape[0] * weighted.shape[1], -1)
    flat_states = qp_states.reshape(qp_states.shape[0], -1)
    result = lax.psum_scatter(
        jnp.dot(flat_states, flat_weighted.T, preferred_element_type=jnp.float32),
        "grid",
        scatter_dimension=0,
        tiled=True,
    )
    return result[None]


def solution(mesh):
    in_specs = (
        P("grp", None, None, "grid", None, None),
        P("grid", None, None),
        P("grp", "grid", None, None),
        P(None, "grid", None, None),
    )
    out_specs = P("grp", "grid", None)
    return jax.shard_map(
        on_device, mesh=mesh, in_specs=in_specs, out_specs=out_specs, check_vma=False
    )
```

profile of v0, /device:TPU:28, one launch (start us, length us, event | category | flops | bytes accessed | tf_op | source)
XLA Modules:
  0.0 656.1 jit_solution(16886512140315843217)
XLA Ops:
  0.0 3.6 constant_dynamic-update-slice_fusion.1
  5.7 4.5 copy-done.4
  15.9 64.2 %collective-permute-done = f32[2,3,2,1,256,256]{5,4,3,2,1,0:T(8,128)} collective-permute-done((f32[2,3,2,1,256,256]{5,4,3,2,1,0:T(8,128)S(1)}, f32[2,3,2,1,256,256]{5,4,3,2,1,0:T(8,128)}, u32[]{:S(2)}, u32[]{:S(2)}) %collective-permute-start) | collective-permute-done | bytes 3145760 | tf_op jit(solution)/shard_map/ppermute | solution.py:19
  83.2 33.2 %fusion.4 = f32[2,3,2,4,256,256]{5,4,3,2,1,0:T(8,128)} fusion(f32[2,3,2,4,256,256]{5,4,3,2,1,0:T(8,128)} %copy-done.4, f32[2,3,2,1,256,256]{5,4,3,2,1,0:T(8,128)} %collective-permute-done.1, f32[2,3,2,1,256,256]{5,4,3,2,1,0:T(8,128)} %collective-permute-done, f32[2,4,256,256]{3,2,1,0:T(8,128)S(1)} %pad_maximum_fusion.17), kind=kLoop, calls=%fused_computation.27 | loop fusion | flops 37748736 | bytes 33554432 | tf_op jit(solution)/shard_map/add | solution.py:96
  116.4 8.8 %slice_multiply_fusion.8 = (f32[2,3,1,4,256,256]{5,4,3,2,1,0:T(8,128)S(1)}, f32[2,3,1,4,256,256]{5,4,3,2,1,0:T(8,128)}) fusion(f32[2,3,2,4,256,256]{5,4,3,2,1,0:T(8,128)} %fusion.4), kind=kLoop, calls=%fused_computation.80 | loop fusion | flops 3145728 | bytes 25165824 | tf_op jit(solution)/shard_map/mul | solution.py:56
  125.1 7.3 %fusion.38 = (f32[2,3,2,1,256,256]{5,4,3,2,1,0:T(8,128)}, f32[2,3,2,1,256,256]{5,4,3,2,1,0:T(8,128)}) fusion(f32[2,3,1,4,256,256]{5,4,3,2,1,0:T(8,128)S(1)} %get-tuple-element.17, f32[2,3,1,4,256,256]{5,4,3,2,1,0:T(8,128)} %get-tuple-element.18), kind=kLoop, calls=%fused_computation.86 | loop fusion | flops 1572864 | bytes 18874368 | tf_op jit(solution)/shard_map/stack | solution.py:56
  136.8 8.7 %pad_maximum_fusion = f32[2,3,2,4,256,256]{5,4,3,2,1,0:T(8,128)} fusion(f32[2,3,1,4,256,256]{5,4,3,2,1,0:T(8,128)} %get-tuple-element.18, f32[2,3,1,4,256,256]{5,4,3,2,1,0:T(8,128)S(1)} %get-tuple-element.17), kind=kLoop, calls=%fused_computation.10 | loop fusion | flops 3145728 | bytes 25165824 | tf_op jit(solution)/shard_map/stack | solution.py:56
  145.5 54.8 %collective-permute-done.2 = f32[2,3,2,1,256,256]{5,4,3,2,1,0:T(8,128)} collective-permute-done((f32[2,3,2,1,256,256]{5,4,3,2,1,0:T(8,128)}, f32[2,3,2,1,256,256]{5,4,3,2,1,0:T(8,128)}, u32[]{:S(2)}, u32[]{:S(2)}) %collective-permute-start.2) | collective-permute-done | bytes 3145760 | tf_op jit(solution)/shard_map/ppermute | solution.py:19
  201.4 34.5 %fusion.9 = f32[2,3,2,4,256,256]{5,4,3,2,1,0:T(8,128)} fusion(f32[2,3,2,4,256,256]{5,4,3,2,1,0:T(8,128)} %pad_maximum_fusion, f32[2,3,2,1,256,256]{5,4,3,2,1,0:T(8,128)} %collective-permute-done.3, f32[2,3,1,4,256,256]{5,4,3,2,1,0:T(8,128)} %get-tuple-element.18, f32[2,3,1,4,256,256]{5,4,3,2,1,0:T(8,128)} %copy-done, ...), kind=kLoop, calls=%fused_computation.32 | loop fusion | flops 44040192 | bytes 46137344 | tf_op jit(solution)/shard_map/add | solution.py:96
  235.8 8.8 %slice_multiply_fusion.6 = (f32[2,3,1,4,256,256]{5,4,3,2,1,0:T(8,128)S(1)}, f32[2,3,1,4,256,256]{5,4,3,2,1,0:T(8,128)}) fusion(f32[2,3,2,4,256,256]{5,4,3,2,1,0:T(8,128)} %fusion.9), kind=kLoop, calls=%fused_computation.78 | loop fusion | flops 3145728 | bytes 25165824 | tf_op jit(solution)/shard_map/mul | solution.py:56
  244.6 7.5 %fusion.36 = (f32[2,3,2,1,256,256]{5,4,3,2,1,0:T(8,128)}, f32[2,3,2,1,256,256]{5,4,3,2,1,0:T(8,128)}) fusion(f32[2,3,1,4,256,256]{5,4,3,2,1,0:T(8,128)S(1)} %get-tuple-element.13, f32[2,3,1,4,256,256]{5,4,3,2,1,0:T(8,128)} %get-tuple-element.14), kind=kLoop, calls=%fused_computation.84 | loop fusion | flops 1572864 | bytes 18874368 | tf_op jit(solution)/shard_map/stack | solution.py:56
  252.1 3.7 collective-permute-start.4
  258.0 8.8 %pad_maximum_fusion.1 = f32[2,3,2,4,256,256]{5,4,3,2,1,0:T(8,128)} fusion(f32[2,3,1,4,256,256]{5,4,3,2,1,0:T(8,128)} %get-tuple-element.14, f32[2,3,1,4,256,256]{5,4,3,2,1,0:T(8,128)S(1)} %get-tuple-element.13), kind=kLoop, calls=%fused_computation.15 | loop fusion | flops 3145728 | bytes 25165824 | tf_op jit(solution)/shard_map/stack | solution.py:56
  266.8 53.9 %collective-permute-done.4 = f32[2,3,2,1,256,256]{5,4,3,2,1,0:T(8,128)} collective-permute-done((f32[2,3,2,1,256,256]{5,4,3,2,1,0:T(8,128)}, f32[2,3,2,1,256,256]{5,4,3,2,1,0:T(8,128)}, u32[]{:S(2)}, u32[]{:S(2)}) %collective-permute-start.4) | collective-permute-done | bytes 3145760 | tf_op jit(solution)/shard_map/ppermute | solution.py:19
  320.8 34.4 %fusion.14 = f32[2,3,2,4,256,256]{5,4,3,2,1,0:T(8,128)} fusion(f32[2,3,2,4,256,256]{5,4,3,2,1,0:T(8,128)} %pad_maximum_fusion.1, f32[2,3,2,1,256,256]{5,4,3,2,1,0:T(8,128)} %collective-permute-done.5, f32[2,3,1,4,256,256]{5,4,3,2,1,0:T(8,128)} %get-tuple-element.14, f32[2,3,1,4,256,256]{5,4,3,2,1,0:T(8,128)} %copy-done.1, ...), kind=kLoop, calls=%fused_computation.37 | loop fusion | flops 44040192 | bytes 46137344 | tf_op jit(solution)/shard_map/add | solution.py:96
  355.2 8.7 %slice_multiply_fusion.4 = (f32[2,3,1,4,256,256]{5,4,3,2,1,0:T(8,128)S(1)}, f32[2,3,1,4,256,256]{5,4,3,2,1,0:T(8,128)}) fusion(f32[2,3,2,4,256,256]{5,4,3,2,1,0:T(8,128)} %fusion.14), kind=kLoop, calls=%fused_computation.76 | loop fusion | flops 3145728 | bytes 25165824 | tf_op jit(solution)/shard_map/mul | solution.py:56
  363.9 7.4 %fusion.34 = (f32[2,3,2,1,256,256]{5,4,3,2,1,0:T(8,128)}, f32[2,3,2,1,256,256]{5,4,3,2,1,0:T(8,128)}) fusion(f32[2,3,1,4,256,256]{5,4,3,2,1,0:T(8,128)S(1)} %get-tuple-element.9, f32[2,3,1,4,256,256]{5,4,3,2,1,0:T(8,128)} %get-tuple-element.10), kind=kLoop, calls=%fused_computation.82 | loop fusion | flops 1572864 | bytes 18874368 | tf_op jit(solution)/shard_map/stack | solution.py:56
  371.3 4.7 collective-permute-start.6
  379.1 8.8 %pad_maximum_fusion.2 = f32[2,3,2,4,256,256]{5,4,3,2,1,0:T(8,128)} fusion(f32[2,3,1,4,256,256]{5,4,3,2,1,0:T(8,128)} %get-tuple-element.10, f32[2,3,1,4,256,256]{5,4,3,2,1,0:T(8,128)S(1)} %get-tuple-element.9), kind=kLoop, calls=%fused_computation.20 | loop fusion | flops 3145728 | bytes 25165824 | tf_op jit(solution)/shard_map/stack | solution.py:56
  387.9 52.1 %collective-permute-done.6 = f32[2,3,2,1,256,256]{5,4,3,2,1,0:T(8,128)} collective-permute-done((f32[2,3,2,1,256,256]{5,4,3,2,1,0:T(8,128)}, f32[2,3,2,1,256,256]{5,4,3,2,1,0:T(8,128)}, u32[]{:S(2)}, u32[]{:S(2)}) %collective-permute-start.6) | collective-permute-done | bytes 3145760 | tf_op jit(solution)/shard_map/ppermute | solution.py:19
  440.0 34.5 %fusion.19 = f32[2,3,2,4,256,256]{5,4,3,2,1,0:T(8,128)} fusion(f32[2,3,2,4,256,256]{5,4,3,2,1,0:T(8,128)} %pad_maximum_fusion.2, f32[2,3,2,1,256,256]{5,4,3,2,1,0:T(8,128)} %collective-permute-done.7, f32[2,3,1,4,256,256]{5,4,3,2,1,0:T(8,128)} %get-tuple-element.10, f32[2,3,1,4,256,256]{5,4,3,2,1,0:T(8,128)} %copy-done.2, ...), kind=kLoop, calls=%fused_computation.42 | loop fusion | flops 44040192 | bytes 46137344 | tf_op jit(solution)/shard_map/add | solution.py:96
  474.5 11.2 %slice_multiply_fusion.2 = (f32[2,3,1,4,256,256]{5,4,3,2,1,0:T(8,128)}, f32[2,3,1,4,256,256]{5,4,3,2,1,0:T(8,128)}) fusion(f32[2,3,2,4,256,256]{5,4,3,2,1,0:T(8,128)} %fusion.19), kind=kLoop, calls=%fused_computation.74 | loop fusion | flops 3145728 | bytes 25165824 | tf_op jit(solution)/shard_map/mul | solution.py:56
  485.7 24.1 %maximum_add_fusion = f32[2,3,2,4,256,256]{5,4,3,2,1,0:T(8,128)} fusion(f32[2,3,1,4,256,256]{5,4,3,2,1,0:T(8,128)} %get-tuple-element.6, f32[2,3,1,4,256,256]{5,4,3,2,1,0:T(8,128)} %get-tuple-element.5, f32[2,3,2,4,256,256]{5,4,3,2,1,0:T(8,128)} %copy-done.4, f32[2,3,1,4,256,256]{5,4,3,2,1,0:T(8,128)} %get-tuple-element.10, ...), kind=kLoop, calls=%fused_computation.69 | loop fusion | flops 25165824 | bytes 75497472 | tf_op jit(solution)/shard_map/add | solution.py:98
  509.8 6.0 fusion.33
  521.6 10.5 %all-to-all-start = ((f32[4,256,256]{2,0,1:T(4,128)}), f32[4,256,256]{2,0,1:T(4,128)S(1)}, u32[]{:S(2)}, u32[]{:S(2)}) async-start(f32[4,256,256]{2,0,1:T(4,128)} %copy.18), calls=%async_computation | async-start | bytes 2097152 | tf_op jit(solution)/shard_map/all_to_all | solution.py:70
  532.4 13.6 %all-to-all-done = f32[4,256,256]{2,0,1:T(4,128)S(1)} async-done(((f32[4,256,256]{2,0,1:T(4,128)}), f32[4,256,256]{2,0,1:T(4,128)S(1)}, u32[]{:S(2)}, u32[]{:S(2)}) %all-to-all-start) | async-done | bytes 1048608 | tf_op jit(solution)/shard_map/all_to_all | solution.py:70
  549.9 17.7 %all_to_all.36 = f32[32,32,256]{2,1,0:T(8,128)S(1)} all-to-all(f32[32,32,256]{2,1,0:T(8,128)S(1)} %copy.22), channel_id=1, replica_groups=mesh['grp'=4,'grid'=8] {'grid'}, dimensions={0} | all-to-all | bytes 2097152 | tf_op jit(solution)/shard_map/all_to_all | solution.py:83
  573.3 18.2 %copy.32 = bf16[4,8,1024,256]{3,1,2,0:T(8,128)(2,1)} copy(bf16[4,8,1024,256]{3,2,1,0:T(8,128)(2,1)} %bitcast.51) | data formatting | bytes 33554432
  592.7 28.7 %collective-permute-done.8 = f32[4,256,256]{2,1,0:T(8,128)S(1)} collective-permute-done((f32[4,256,256]{2,1,0:T(8,128)S(1)}, f32[4,256,256]{2,1,0:T(8,128)S(1)}, u32[]{:S(2)}, u32[]{:S(2)}) %collective-permute-start.8) | collective-permute-done | bytes 1048608 | tf_op jit(solution)/shard_map/ppermute | solution.py:27
  625.0 5.2 convert_element_type.54
  630.2 11.5 %convolution_bitcast_fusion.2 = f32[32,6]{0,1:T(8,128)S(1)} fusion(bf16[6,262144]{1,0:T(8,128)(2,1)} %convert_element_type.54, bf16[32,262144]{1,0:T(8,128)(2,1)} %bitcast.50), kind=kOutput, calls=%fused_computation.92 | convolution fusion | flops 100663296 | bytes 19923712 | tf_op jit(solution)/shard_map/dot_general | solution.py:106
  641.7 13.5 %all-reduce.8 = f32[32,6]{0,1:T(8,128)S(1)} all-reduce(f32[32,6]{0,1:T(8,128)S(1)} %convolution_bitcast_fusion.2), channel_id=2, replica_groups=mesh['grp'=4,'grid'=8] {'grid'}, use_global_device_ids=true, to_apply=%region_1.2.clone | all-reduce | flops 192 | bytes 1536
  (58 shorter events, 41.9 us)
Async XLA Ops:
  0.0 4.6 copy-start.6
  4.6 10.9 %copy-start.7 = (f32[1,4,256,256]{3,2,1,0:T(8,128)S(1)}, f32[1,4,256,256]{3,2,1,0:T(8,128)}, u32[]{:S(2)}) copy-start(f32[1,4,256,256]{3,2,1,0:T(8,128)} %param.6) | copy-start | bytes 3145732
  4.6 10.9 %copy-start.9 = (f32[4,256,256]{2,1,0:T(8,128)S(1)}, f32[4,256,256]{2,1,0:T(8,128)}, u32[]{:S(2)}) copy-start(f32[4,256,256]{2,1,0:T(8,128)} %param.5) | copy-start | bytes 3145732
  5.7 4.5 copy-start.4
  10.8 69.3 %collective-permute-start = (f32[2,3,2,1,256,256]{5,4,3,2,1,0:T(8,128)S(1)}, f32[2,3,2,1,256,256]{5,4,3,2,1,0:T(8,128)}, u32[]{:S(2)}, u32[]{:S(2)}) collective-permute-start(f32[2,3,2,1,256,256]{5,4,3,2,1,0:T(8,128)S(1)} %get-tuple-element.19), channel_id=1, source_target_pairs={{1,0},{2,1},{3,2},{4,3},{5,4},{6,5},{7,6},{9,8},{10,9},{11,10},{12... | collective-permute-start | bytes 9437192 | tf_op jit(solution)/shard_map/ppermute | solution.py:19
  13.6 69.6 %collective-permute-start.1 = (f32[2,3,2,1,256,256]{5,4,3,2,1,0:T(8,128)S(1)}, f32[2,3,2,1,256,256]{5,4,3,2,1,0:T(8,128)}, u32[]{:S(2)}, u32[]{:S(2)}) collective-permute-start(f32[2,3,2,1,256,256]{5,4,3,2,1,0:T(8,128)S(1)} %get-tuple-element.20), channel_id=1, source_target_pairs={{0,1},{1,2},{2,3},{3,4},{4,5},{5,6},{6,7},{8,9},{9,10},{10,11},{11... | collective-permute-start | bytes 9437192 | tf_op jit(solution)/shard_map/ppermute | solution.py:16
  15.9 67.3 %copy-start.5 = (f32[2,4,256,256]{3,2,1,0:T(8,128)}, f32[2,4,256,256]{3,2,1,0:T(8,128)S(1)}, u32[]{:S(2)}) copy-start(f32[2,4,256,256]{3,2,1,0:T(8,128)S(1)} %pad_maximum_fusion.17) | copy-start | bytes 6291460
  125.1 20.4 %copy-start = (f32[2,3,1,4,256,256]{5,4,3,2,1,0:T(8,128)}, f32[2,3,1,4,256,256]{5,4,3,2,1,0:T(8,128)S(1)}, u32[]{:S(2)}) copy-start(f32[2,3,1,4,256,256]{5,4,3,2,1,0:T(8,128)S(1)} %get-tuple-element.17) | copy-start | bytes 18874372
  132.5 67.9 %collective-permute-start.2 = (f32[2,3,2,1,256,256]{5,4,3,2,1,0:T(8,128)}, f32[2,3,2,1,256,256]{5,4,3,2,1,0:T(8,128)}, u32[]{:S(2)}, u32[]{:S(2)}) collective-permute-start(f32[2,3,2,1,256,256]{5,4,3,2,1,0:T(8,128)} %get-tuple-element.15), channel_id=1, source_target_pairs={{1,0},{2,1},{3,2},{4,3},{5,4},{6,5},{7,6},{9,8},{10,9},{11,10},{12... | collective-permute-start | bytes 9437192 | tf_op jit(solution)/shard_map/ppermute | solution.py:19
  134.4 67.0 %collective-permute-start.3 = (f32[2,3,2,1,256,256]{5,4,3,2,1,0:T(8,128)}, f32[2,3,2,1,256,256]{5,4,3,2,1,0:T(8,128)}, u32[]{:S(2)}, u32[]{:S(2)}) collective-permute-start(f32[2,3,2,1,256,256]{5,4,3,2,1,0:T(8,128)} %get-tuple-element.16), channel_id=1, source_target_pairs={{0,1},{1,2},{2,3},{3,4},{4,5},{5,6},{6,7},{8,9},{9,10},{10,11},{11... | collective-permute-start | bytes 9437192 | tf_op jit(solution)/shard_map/ppermute | solution.py:16
  244.6 22.2 %copy-start.1 = (f32[2,3,1,4,256,256]{5,4,3,2,1,0:T(8,128)}, f32[2,3,1,4,256,256]{5,4,3,2,1,0:T(8,128)S(1)}, u32[]{:S(2)}) copy-start(f32[2,3,1,4,256,256]{5,4,3,2,1,0:T(8,128)S(1)} %get-tuple-element.13) | copy-start | bytes 18874372
  252.1 68.7 %collective-permute-start.4 = (f32[2,3,2,1,256,256]{5,4,3,2,1,0:T(8,128)}, f32[2,3,2,1,256,256]{5,4,3,2,1,0:T(8,128)}, u32[]{:S(2)}, u32[]{:S(2)}) collective-permute-start(f32[2,3,2,1,256,256]{5,4,3,2,1,0:T(8,128)} %get-tuple-element.11), channel_id=1, source_target_pairs={{1,0},{2,1},{3,2},{4,3},{5,4},{6,5},{7,6},{9,8},{10,9},{11,10},{12... | collective-permute-start | bytes 9437192 | tf_op jit(solution)/shard_map/ppermute | solution.py:19
  255.8 65.0 %collective-permute-start.5 = (f32[2,3,2,1,256,256]{5,4,3,2,1,0:T(8,128)}, f32[2,3,2,1,256,256]{5,4,3,2,1,0:T(8,128)}, u32[]{:S(2)}, u32[]{:S(2)}) collective-permute-start(f32[2,3,2,1,256,256]{5,4,3,2,1,0:T(8,128)} %get-tuple-element.12), channel_id=1, source_target_pairs={{0,1},{1,2},{2,3},{3,4},{4,5},{5,6},{6,7},{8,9},{9,10},{10,11},{11... | collective-permute-start | bytes 9437192 | tf_op jit(solution)/shard_map/ppermute | solution.py:16
  363.9 24.0 %copy-start.2 = (f32[2,3,1,4,256,256]{5,4,3,2,1,0:T(8,128)}, f32[2,3,1,4,256,256]{5,4,3,2,1,0:T(8,128)S(1)}, u32[]{:S(2)}) copy-start(f32[2,3,1,4,256,256]{5,4,3,2,1,0:T(8,128)S(1)} %get-tuple-element.9) | copy-start | bytes 18874372
  371.3 68.6 %collective-permute-start.6 = (f32[2,3,2,1,256,256]{5,4,3,2,1,0:T(8,128)}, f32[2,3,2,1,256,256]{5,4,3,2,1,0:T(8,128)}, u32[]{:S(2)}, u32[]{:S(2)}) collective-permute-start(f32[2,3,2,1,256,256]{5,4,3,2,1,0:T(8,128)} %get-tuple-element.7), channel_id=1, source_target_pairs={{1,0},{2,1},{3,2},{4,3},{5,4},{6,5},{7,6},{9,8},{10,9},{11,10},{12... | collective-permute-start | bytes 9437192 | tf_op jit(solution)/shard_map/ppermute | solution.py:19
  376.1 63.9 %collective-permute-start.7 = (f32[2,3,2,1,256,256]{5,4,3,2,1,0:T(8,128)}, f32[2,3,2,1,256,256]{5,4,3,2,1,0:T(8,128)}, u32[]{:S(2)}, u32[]{:S(2)}) collective-permute-start(f32[2,3,2,1,256,256]{5,4,3,2,1,0:T(8,128)} %get-tuple-element.8), channel_id=1, source_target_pairs={{0,1},{1,2},{2,3},{3,4},{4,5},{5,6},{6,7},{8,9},{9,10},{10,11},{11... | collective-permute-start | bytes 9437192 | tf_op jit(solution)/shard_map/ppermute | solution.py:16
  474.5 11.2 %copy-start.3 = (f32[2,3,1,4,256,256]{5,4,3,2,1,0:T(8,128)S(1)}, f32[2,3,1,4,256,256]{5,4,3,2,1,0:T(8,128)}, u32[]{:S(2)}) copy-start(f32[2,3,1,4,256,256]{5,4,3,2,1,0:T(8,128)} %copy-done.2) | copy-start | bytes 18874372
  521.6 24.4 %all-to-all-start = ((f32[4,256,256]{2,0,1:T(4,128)}), f32[4,256,256]{2,0,1:T(4,128)S(1)}, u32[]{:S(2)}, u32[]{:S(2)}) async-start(f32[4,256,256]{2,0,1:T(4,128)} %copy.18), calls=%async_computation | async-start | bytes 2097152 | tf_op jit(solution)/shard_map/all_to_all | solution.py:70
  571.9 49.5 %collective-permute-start.8 = (f32[4,256,256]{2,1,0:T(8,128)S(1)}, f32[4,256,256]{2,1,0:T(8,128)S(1)}, u32[]{:S(2)}, u32[]{:S(2)}) collective-permute-start(f32[4,256,256]{2,1,0:T(8,128)S(1)} %fusion.50), channel_id=1, source_target_pairs={{0,16},{8,24},{1,17},{9,25},{2,18},{10,26},{3,19},{11,27},{4,20},{... | collective-permute-start | bytes 3145736 | tf_op jit(solution)/shard_map/ppermute | solution.py:27
  573.3 18.2 %copy-start.10 = (u32[32]{0:T(128)S(1)}, u32[32]{0:T(128)}, u32[]{:S(2)}) copy-start(u32[32]{0:T(128)} %constant.111) | copy-start | bytes 388
  573.3 48.2 %copy-start.8 = (f32[1,4,256,256]{3,2,1,0:T(8,128)S(1)}, f32[1,4,256,256]{3,2,1,0:T(8,128)}, u32[]{:S(2)}) copy-start(f32[1,4,256,256]{3,2,1,0:T(8,128)} %param.6) | copy-start | bytes 3145732
where the time goes:
time: 665 us; the launch traced here: 656 us
  waiting for transfers between devices  271 us (41%)
  other arithmetic  257 us (39%)
  local copies, waits for them, and re-layouts  38.3 us (6%)
  starting transfers between devices  34.5 us (5%)
  blocking collectives  31.2 us (5%)
  matrix products  22.7 us (3%)
    ppermute x4, waiting for transfers between devices, padded_2(): lax.ppermute(lax.slice_in_dim(block, 0, width, axis=dim), axis, backward)  225 us
    add x4, other arithmetic, on_device(): applied = -0.5 * laplace_inner(padded) + fields[:, None, None] * current  137 us
    another operation x6, other arithmetic, taylor_term(): jnp.stack([factor * applied[:, :, 1], -factor * applied[:, :, 0]], axis=2)  48.5 us
    mul x4, other arithmetic, taylor_term(): factor * applied[:, :, 1]  37.4 us
    ppermute x1, waiting for transfers between devices, shifted(): return lax.ppermute(array, axis, pairs)  28.7 us
    unnamed x26, local copies, waits for them, and re-layouts  28 us
    add x1, other arithmetic, on_device(): summed = summed + current  24.1 us
    all_to_all x1, blocking collectives, poisson_block(): lax.all_to_all(field, 'grid', split_axis=0, concat_axis=1, tiled=True)  17.7 us
  transfers between devices with their start and end apart: 10, of which 8 were waited for; matrix products, arithmetic and copies ran while one was open for 7% of the time, Pallas kernels for 0%

commit v1 on v0

--- a/solution.py
+++ b/solution.py
@@ -67,7 +67,10 @@
     table_z = sine_table(size_z)
     field = jnp.einsum("xyz,zl->xyl", density, table_z, precision=highest)
     field = jnp.einsum("xyl,yk->xkl", field, table_y, precision=highest)
-    columns = lax.all_to_all(field, "grid", split_axis=1, concat_axis=0, tiled=True)
+    columns = jnp.concatenate(
+        lax.all_to_all(jnp.stack(jnp.split(field, lax.axis_size("grid"), axis=1)), "grid", 0, 0),
+        axis=0,
+    )
     row_count = columns.shape[1]
     own_rows = lax.dynamic_slice_in_dim(
         eigenvalues(size_y), lax.axis_index("grid") * row_count, row_count

time: 665 us -> 668 us (level)
    unnamed x26 -> x33, local copies, waits for them, and re-layouts: 28 us -> 32.6 us
where the time goes in v1:
time: 668 us; the launch traced here: 660 us
  waiting for transfers between devices  272 us (41%)
  other arithmetic  257 us (38%)
  local copies, waits for them, and re-layouts  41.6 us (6%)
  starting transfers between devices  34.3 us (5%)
  blocking collectives  31.2 us (5%)
  matrix products  22.7 us (3%)
    ppermute x4, waiting for transfers between devices, padded_2(): lax.ppermute(lax.slice_in_dim(block, 0, width, axis=dim), axis, backward)  225 us
    add x4, other arithmetic, on_device(): applied = -0.5 * laplace_inner(padded) + fields[:, None, None] * current  137 us
    another operation x6, other arithmetic, taylor_term(): jnp.stack([factor * applied[:, :, 1], -factor * applied[:, :, 0]], axis=2)  48.4 us
    mul x4, other arithmetic, taylor_term(): factor * applied[:, :, 1]  37.5 us
    unnamed x33, local copies, waits for them, and re-layouts  32.6 us
    ppermute x1, waiting for transfers between devices, shifted(): return lax.ppermute(array, axis, pairs)  28.7 us
    add x1, other arithmetic, on_device(): summed = summed + current  24.1 us
    all_to_all x1, blocking collectives, poisson_block(): lax.all_to_all(field, 'grid', split_axis=0, concat_axis=1, tiled=True)  17.7 us
  transfers between devices with their start and end apart: 10, of which 8 were waited for; matrix products, arithmetic and copies ran while one was open for 7% of the time, Pallas kernels for 0%

profile of v1, /device:TPU:28, one launch (start us, length us, event | category | flops | bytes accessed | tf_op | source)
XLA Modules:
  0.0 659.6 jit_solution(8340969548988594998)
XLA Ops:
  0.0 3.6 constant_dynamic-update-slice_fusion.1
  5.7 4.5 copy-done.4
  15.9 64.2 %collective-permute-done = f32[2,3,2,1,256,256]{5,4,3,2,1,0:T(8,128)} collective-permute-done((f32[2,3,2,1,256,256]{5,4,3,2,1,0:T(8,128)S(1)}, f32[2,3,2,1,256,256]{5,4,3,2,1,0:T(8,128)}, u32[]{:S(2)}, u32[]{:S(2)}) %collective-permute-start) | collective-permute-done | bytes 3145760 | tf_op jit(solution)/shard_map/ppermute | solution.py:19
  83.2 33.2 %fusion.4 = f32[2,3,2,4,256,256]{5,4,3,2,1,0:T(8,128)} fusion(f32[2,3,2,4,256,256]{5,4,3,2,1,0:T(8,128)} %copy-done.4, f32[2,3,2,1,256,256]{5,4,3,2,1,0:T(8,128)} %collective-permute-done.1, f32[2,3,2,1,256,256]{5,4,3,2,1,0:T(8,128)} %collective-permute-done, f32[2,4,256,256]{3,2,1,0:T(8,128)S(1)} %pad_maximum_fusion.17), kind=kLoop, calls=%fused_computation.27 | loop fusion | flops 37748736 | bytes 33554432 | tf_op jit(solution)/shard_map/add | solution.py:99
  116.4 8.8 %slice_multiply_fusion.8 = (f32[2,3,1,4,256,256]{5,4,3,2,1,0:T(8,128)S(1)}, f32[2,3,1,4,256,256]{5,4,3,2,1,0:T(8,128)}) fusion(f32[2,3,2,4,256,256]{5,4,3,2,1,0:T(8,128)} %fusion.4), kind=kLoop, calls=%fused_computation.80 | loop fusion | flops 3145728 | bytes 25165824 | tf_op jit(solution)/shard_map/mul | solution.py:56
  125.1 7.3 %fusion.38 = (f32[2,3,2,1,256,256]{5,4,3,2,1,0:T(8,128)}, f32[2,3,2,1,256,256]{5,4,3,2,1,0:T(8,128)}) fusion(f32[2,3,1,4,256,256]{5,4,3,2,1,0:T(8,128)S(1)} %get-tuple-element.17, f32[2,3,1,4,256,256]{5,4,3,2,1,0:T(8,128)} %get-tuple-element.18), kind=kLoop, calls=%fused_computation.86 | loop fusion | flops 1572864 | bytes 18874368 | tf_op jit(solution)/shard_map/stack | solution.py:56
  136.8 8.7 %pad_maximum_fusion = f32[2,3,2,4,256,256]{5,4,3,2,1,0:T(8,128)} fusion(f32[2,3,1,4,256,256]{5,4,3,2,1,0:T(8,128)} %get-tuple-element.18, f32[2,3,1,4,256,256]{5,4,3,2,1,0:T(8,128)S(1)} %get-tuple-element.17), kind=kLoop, calls=%fused_computation.10 | loop fusion | flops 3145728 | bytes 25165824 | tf_op jit(solution)/shard_map/stack | solution.py:56
  145.5 54.8 %collective-permute-done.2 = f32[2,3,2,1,256,256]{5,4,3,2,1,0:T(8,128)} collective-permute-done((f32[2,3,2,1,256,256]{5,4,3,2,1,0:T(8,128)}, f32[2,3,2,1,256,256]{5,4,3,2,1,0:T(8,128)}, u32[]{:S(2)}, u32[]{:S(2)}) %collective-permute-start.2) | collective-permute-done | bytes 3145760 | tf_op jit(solution)/shard_map/ppermute | solution.py:19
  201.4 34.5 %fusion.9 = f32[2,3,2,4,256,256]{5,4,3,2,1,0:T(8,128)} fusion(f32[2,3,2,4,256,256]{5,4,3,2,1,0:T(8,128)} %pad_maximum_fusion, f32[2,3,2,1,256,256]{5,4,3,2,1,0:T(8,128)} %collective-permute-done.3, f32[2,3,1,4,256,256]{5,4,3,2,1,0:T(8,128)} %get-tuple-element.18, f32[2,3,1,4,256,256]{5,4,3,2,1,0:T(8,128)} %copy-done, ...), kind=kLoop, calls=%fused_computation.32 | loop fusion | flops 44040192 | bytes 46137344 | tf_op jit(solution)/shard_map/add | solution.py:99
  235.8 8.8 %slice_multiply_fusion.6 = (f32[2,3,1,4,256,256]{5,4,3,2,1,0:T(8,128)S(1)}, f32[2,3,1,4,256,256]{5,4,3,2,1,0:T(8,128)}) fusion(f32[2,3,2,4,256,256]{5,4,3,2,1,0:T(8,128)} %fusion.9), kind=kLoop, calls=%fused_computation.78 | loop fusion | flops 3145728 | bytes 25165824 | tf_op jit(solution)/shard_map/mul | solution.py:56
  244.6 7.5 %fusion.36 = (f32[2,3,2,1,256,256]{5,4,3,2,1,0:T(8,128)}, f32[2,3,2,1,256,256]{5,4,3,2,1,0:T(8,128)}) fusion(f32[2,3,1,4,256,256]{5,4,3,2,1,0:T(8,128)S(1)} %get-tuple-element.13, f32[2,3,1,4,256,256]{5,4,3,2,1,0:T(8,128)} %get-tuple-element.14), kind=kLoop, calls=%fused_computation.84 | loop fusion | flops 1572864 | bytes 18874368 | tf_op jit(solution)/shard_map/stack | solution.py:56
  252.1 3.7 collective-permute-start.4
  258.0 8.8 %pad_maximum_fusion.1 = f32[2,3,2,4,256,256]{5,4,3,2,1,0:T(8,128)} fusion(f32[2,3,1,4,256,256]{5,4,3,2,1,0:T(8,128)} %get-tuple-element.14, f32[2,3,1,4,256,256]{5,4,3,2,1,0:T(8,128)S(1)} %get-tuple-element.13), kind=kLoop, calls=%fused_computation.15 | loop fusion | flops 3145728 | bytes 25165824 | tf_op jit(solution)/shard_map/stack | solution.py:56
  266.8 54.0 %collective-permute-done.4 = f32[2,3,2,1,256,256]{5,4,3,2,1,0:T(8,128)} collective-permute-done((f32[2,3,2,1,256,256]{5,4,3,2,1,0:T(8,128)}, f32[2,3,2,1,256,256]{5,4,3,2,1,0:T(8,128)}, u32[]{:S(2)}, u32[]{:S(2)}) %collective-permute-start.4) | collective-permute-done | bytes 3145760 | tf_op jit(solution)/shard_map/ppermute | solution.py:19
  320.8 34.4 %fusion.14 = f32[2,3,2,4,256,256]{5,4,3,2,1,0:T(8,128)} fusion(f32[2,3,2,4,256,256]{5,4,3,2,1,0:T(8,128)} %pad_maximum_fusion.1, f32[2,3,2,1,256,256]{5,4,3,2,1,0:T(8,128)} %collective-permute-done.5, f32[2,3,1,4,256,256]{5,4,3,2,1,0:T(8,128)} %get-tuple-element.14, f32[2,3,1,4,256,256]{5,4,3,2,1,0:T(8,128)} %copy-done.1, ...), kind=kLoop, calls=%fused_computation.37 | loop fusion | flops 44040192 | bytes 46137344 | tf_op jit(solution)/shard_map/add | solution.py:99
  355.2 8.8 %slice_multiply_fusion.4 = (f32[2,3,1,4,256,256]{5,4,3,2,1,0:T(8,128)S(1)}, f32[2,3,1,4,256,256]{5,4,3,2,1,0:T(8,128)}) fusion(f32[2,3,2,4,256,256]{5,4,3,2,1,0:T(8,128)} %fusion.14), kind=kLoop, calls=%fused_computation.76 | loop fusion | flops 3145728 | bytes 25165824 | tf_op jit(solution)/shard_map/mul | solution.py:56
  364.0 7.4 %fusion.34 = (f32[2,3,2,1,256,256]{5,4,3,2,1,0:T(8,128)}, f32[2,3,2,1,256,256]{5,4,3,2,1,0:T(8,128)}) fusion(f32[2,3,1,4,256,256]{5,4,3,2,1,0:T(8,128)S(1)} %get-tuple-element.9, f32[2,3,1,4,256,256]{5,4,3,2,1,0:T(8,128)} %get-tuple-element.10), kind=kLoop, calls=%fused_computation.82 | loop fusion | flops 1572864 | bytes 18874368 | tf_op jit(solution)/shard_map/stack | solution.py:56
  371.4 4.7 collective-permute-start.6
  379.2 8.7 %pad_maximum_fusion.2 = f32[2,3,2,4,256,256]{5,4,3,2,1,0:T(8,128)} fusion(f32[2,3,1,4,256,256]{5,4,3,2,1,0:T(8,128)} %get-tuple-element.10, f32[2,3,1,4,256,256]{5,4,3,2,1,0:T(8,128)S(1)} %get-tuple-element.9), kind=kLoop, calls=%fused_computation.20 | loop fusion | flops 3145728 | bytes 25165824 | tf_op jit(solution)/shard_map/stack | solution.py:56
  387.9 52.2 %collective-permute-done.6 = f32[2,3,2,1,256,256]{5,4,3,2,1,0:T(8,128)} collective-permute-done((f32[2,3,2,1,256,256]{5,4,3,2,1,0:T(8,128)}, f32[2,3,2,1,256,256]{5,4,3,2,1,0:T(8,128)}, u32[]{:S(2)}, u32[]{:S(2)}) %collective-permute-start.6) | collective-permute-done | bytes 3145760 | tf_op jit(solution)/shard_map/ppermute | solution.py:19
  440.0 34.5 %fusion.19 = f32[2,3,2,4,256,256]{5,4,3,2,1,0:T(8,128)} fusion(f32[2,3,2,4,256,256]{5,4,3,2,1,0:T(8,128)} %pad_maximum_fusion.2, f32[2,3,2,1,256,256]{5,4,3,2,1,0:T(8,128)} %collective-permute-done.7, f32[2,3,1,4,256,256]{5,4,3,2,1,0:T(8,128)} %get-tuple-element.10, f32[2,3,1,4,256,256]{5,4,3,2,1,0:T(8,128)} %copy-done.2, ...), kind=kLoop, calls=%fused_computation.42 | loop fusion | flops 44040192 | bytes 46137344 | tf_op jit(solution)/shard_map/add | solution.py:99
  474.6 11.2 %slice_multiply_fusion.2 = (f32[2,3,1,4,256,256]{5,4,3,2,1,0:T(8,128)}, f32[2,3,1,4,256,256]{5,4,3,2,1,0:T(8,128)}) fusion(f32[2,3,2,4,256,256]{5,4,3,2,1,0:T(8,128)} %fusion.19), kind=kLoop, calls=%fused_computation.74 | loop fusion | flops 3145728 | bytes 25165824 | tf_op jit(solution)/shard_map/mul | solution.py:56
  485.7 24.1 %maximum_add_fusion = f32[2,3,2,4,256,256]{5,4,3,2,1,0:T(8,128)} fusion(f32[2,3,1,4,256,256]{5,4,3,2,1,0:T(8,128)} %get-tuple-element.6, f32[2,3,1,4,256,256]{5,4,3,2,1,0:T(8,128)} %get-tuple-element.5, f32[2,3,2,4,256,256]{5,4,3,2,1,0:T(8,128)} %copy-done.4, f32[2,3,1,4,256,256]{5,4,3,2,1,0:T(8,128)} %get-tuple-element.10, ...), kind=kLoop, calls=%fused_computation.69 | loop fusion | flops 25165824 | bytes 75497472 | tf_op jit(solution)/shard_map/add | solution.py:101
  509.8 6.0 fusion.33
  525.3 10.3 %all-to-all-start = ((f32[8,4,32,256]{3,2,1,0:T(8,128)}), f32[8,4,32,256]{3,2,1,0:T(8,128)S(1)}, u32[]{:S(2)}, u32[]{:S(2)}) async-start(f32[8,4,32,256]{3,2,1,0:T(8,128)} %fusion.56), calls=%async_computation | async-start | bytes 2097152 | tf_op jit(solution)/shard_map/all_to_all | solution.py:71
  535.9 13.6 %all-to-all-done = f32[8,4,32,256]{3,2,1,0:T(8,128)S(1)} async-done(((f32[8,4,32,256]{3,2,1,0:T(8,128)}), f32[8,4,32,256]{3,2,1,0:T(8,128)S(1)}, u32[]{:S(2)}, u32[]{:S(2)}) %all-to-all-start) | async-done | bytes 1048608 | tf_op jit(solution)/shard_map/all_to_all | solution.py:71
  553.1 17.7 %all_to_all.23 = f32[32,32,256]{2,1,0:T(8,128)S(1)} all-to-all(f32[32,32,256]{2,1,0:T(8,128)S(1)} %copy.17), channel_id=1, replica_groups=mesh['grp'=4,'grid'=8] {'grid'}, dimensions={0} | all-to-all | bytes 2097152 | tf_op jit(solution)/shard_map/all_to_all | solution.py:86
  576.5 18.2 %copy.27 = bf16[4,8,1024,256]{3,1,2,0:T(8,128)(2,1)} copy(bf16[4,8,1024,256]{3,2,1,0:T(8,128)(2,1)} %bitcast.80) | data formatting | bytes 33554432
  595.9 28.7 %collective-permute-done.8 = f32[4,256,256]{2,1,0:T(8,128)S(1)} collective-permute-done((f32[4,256,256]{2,1,0:T(8,128)S(1)}, f32[4,256,256]{2,1,0:T(8,128)S(1)}, u32[]{:S(2)}, u32[]{:S(2)}) %collective-permute-start.8) | collective-permute-done | bytes 1048608 | tf_op jit(solution)/shard_map/ppermute | solution.py:27
  628.2 5.2 convert_element_type.54
  633.4 11.5 %convolution_bitcast_fusion.2 = f32[32,6]{0,1:T(8,128)S(1)} fusion(bf16[6,262144]{1,0:T(8,128)(2,1)} %convert_element_type.54, bf16[32,262144]{1,0:T(8,128)(2,1)} %bitcast.79), kind=kOutput, calls=%fused_computation.92 | convolution fusion | flops 100663296 | bytes 19923712 | tf_op jit(solution)/shard_map/dot_general | solution.py:109
  644.9 13.5 %all-reduce.8 = f32[32,6]{0,1:T(8,128)S(1)} all-reduce(f32[32,6]{0,1:T(8,128)S(1)} %convolution_bitcast_fusion.2), channel_id=2, replica_groups=mesh['grp'=4,'grid'=8] {'grid'}, use_global_device_ids=true, to_apply=%region_1.2.clone | all-reduce | flops 192 | bytes 1536
  (63 shorter events, 45.2 us)
Async XLA Ops:
  0.0 4.6 copy-start.6
  4.6 10.9 %copy-start.7 = (f32[1,4,256,256]{3,2,1,0:T(8,128)S(1)}, f32[1,4,256,256]{3,2,1,0:T(8,128)}, u32[]{:S(2)}) copy-start(f32[1,4,256,256]{3,2,1,0:T(8,128)} %param.6) | copy-start | bytes 3145732
  4.6 10.9 %copy-start.9 = (f32[4,256,256]{2,1,0:T(8,128)S(1)}, f32[4,256,256]{2,1,0:T(8,128)}, u32[]{:S(2)}) copy-start(f32[4,256,256]{2,1,0:T(8,128)} %param.5) | copy-start | bytes 3145732
  5.7 4.5 copy-start.4
  10.8 69.3 %collective-permute-start = (f32[2,3,2,1,256,256]{5,4,3,2,1,0:T(8,128)S(1)}, f32[2,3,2,1,256,256]{5,4,3,2,1,0:T(8,128)}, u32[]{:S(2)}, u32[]{:S(2)}) collective-permute-start(f32[2,3,2,1,256,256]{5,4,3,2,1,0:T(8,128)S(1)} %get-tuple-element.19), channel_id=1, source_target_pairs={{1,0},{2,1},{3,2},{4,3},{5,4},{6,5},{7,6},{9,8},{10,9},{11,10},{12... | collective-permute-start | bytes 9437192 | tf_op jit(solution)/shard_map/ppermute | solution.py:19
  13.6 69.6 %collective-permute-start.1 = (f32[2,3,2,1,256,256]{5,4,3,2,1,0:T(8,128)S(1)}, f32[2,3,2,1,256,256]{5,4,3,2,1,0:T(8,128)}, u32[]{:S(2)}, u32[]{:S(2)}) collective-permute-start(f32[2,3,2,1,256,256]{5,4,3,2,1,0:T(8,128)S(1)} %get-tuple-element.20), channel_id=1, source_target_pairs={{0,1},{1,2},{2,3},{3,4},{4,5},{5,6},{6,7},{8,9},{9,10},{10,11},{11... | collective-permute-start | bytes 9437192 | tf_op jit(solution)/shard_map/ppermute | solution.py:16
  15.9 67.3 %copy-start.5 = (f32[2,4,256,256]{3,2,1,0:T(8,128)}, f32[2,4,256,256]{3,2,1,0:T(8,128)S(1)}, u32[]{:S(2)}) copy-start(f32[2,4,256,256]{3,2,1,0:T(8,128)S(1)} %pad_maximum_fusion.17) | copy-start | bytes 6291460
  125.1 20.4 %copy-start = (f32[2,3,1,4,256,256]{5,4,3,2,1,0:T(8,128)}, f32[2,3,1,4,256,256]{5,4,3,2,1,0:T(8,128)S(1)}, u32[]{:S(2)}) copy-start(f32[2,3,1,4,256,256]{5,4,3,2,1,0:T(8,128)S(1)} %get-tuple-element.17) | copy-start | bytes 18874372
  132.5 67.9 %collective-permute-start.2 = (f32[2,3,2,1,256,256]{5,4,3,2,1,0:T(8,128)}, f32[2,3,2,1,256,256]{5,4,3,2,1,0:T(8,128)}, u32[]{:S(2)}, u32[]{:S(2)}) collective-permute-start(f32[2,3,2,1,256,256]{5,4,3,2,1,0:T(8,128)} %get-tuple-element.15), channel_id=1, source_target_pairs={{1,0},{2,1},{3,2},{4,3},{5,4},{6,5},{7,6},{9,8},{10,9},{11,10},{12... | collective-permute-start | bytes 9437192 | tf_op jit(solution)/shard_map/ppermute | solution.py:19
  134.4 67.0 %collective-permute-start.3 = (f32[2,3,2,1,256,256]{5,4,3,2,1,0:T(8,128)}, f32[2,3,2,1,256,256]{5,4,3,2,1,0:T(8,128)}, u32[]{:S(2)}, u32[]{:S(2)}) collective-permute-start(f32[2,3,2,1,256,256]{5,4,3,2,1,0:T(8,128)} %get-tuple-element.16), channel_id=1, source_target_pairs={{0,1},{1,2},{2,3},{3,4},{4,5},{5,6},{6,7},{8,9},{9,10},{10,11},{11... | collective-permute-start | bytes 9437192 | tf_op jit(solution)/shard_map/ppermute | solution.py:16
  244.6 22.2 %copy-start.1 = (f32[2,3,1,4,256,256]{5,4,3,2,1,0:T(8,128)}, f32[2,3,1,4,256,256]{5,4,3,2,1,0:T(8,128)S(1)}, u32[]{:S(2)}) copy-start(f32[2,3,1,4,256,256]{5,4,3,2,1,0:T(8,128)S(1)} %get-tuple-element.13) | copy-start | bytes 18874372
  252.1 68.7 %collective-permute-start.4 = (f32[2,3,2,1,256,256]{5,4,3,2,1,0:T(8,128)}, f32[2,3,2,1,256,256]{5,4,3,2,1,0:T(8,128)}, u32[]{:S(2)}, u32[]{:S(2)}) collective-permute-start(f32[2,3,2,1,256,256]{5,4,3,2,1,0:T(8,128)} %get-tuple-element.11), channel_id=1, source_target_pairs={{1,0},{2,1},{3,2},{4,3},{5,4},{6,5},{7,6},{9,8},{10,9},{11,10},{12... | collective-permute-start | bytes 9437192 | tf_op jit(solution)/shard_map/ppermute | solution.py:19
  255.8 65.0 %collective-permute-start.5 = (f32[2,3,2,1,256,256]{5,4,3,2,1,0:T(8,128)}, f32[2,3,2,1,256,256]{5,4,3,2,1,0:T(8,128)}, u32[]{:S(2)}, u32[]{:S(2)}) collective-permute-start(f32[2,3,2,1,256,256]{5,4,3,2,1,0:T(8,128)} %get-tuple-element.12), channel_id=1, source_target_pairs={{0,1},{1,2},{2,3},{3,4},{4,5},{5,6},{6,7},{8,9},{9,10},{10,11},{11... | collective-permute-start | bytes 9437192 | tf_op jit(solution)/shard_map/ppermute | solution.py:16
  364.0 23.9 %copy-start.2 = (f32[2,3,1,4,256,256]{5,4,3,2,1,0:T(8,128)}, f32[2,3,1,4,256,256]{5,4,3,2,1,0:T(8,128)S(1)}, u32[]{:S(2)}) copy-start(f32[2,3,1,4,256,256]{5,4,3,2,1,0:T(8,128)S(1)} %get-tuple-element.9) | copy-start | bytes 18874372
  371.4 68.6 %collective-permute-start.6 = (f32[2,3,2,1,256,256]{5,4,3,2,1,0:T(8,128)}, f32[2,3,2,1,256,256]{5,4,3,2,1,0:T(8,128)}, u32[]{:S(2)}, u32[]{:S(2)}) collective-permute-start(f32[2,3,2,1,256,256]{5,4,3,2,1,0:T(8,128)} %get-tuple-element.7), channel_id=1, source_target_pairs={{1,0},{2,1},{3,2},{4,3},{5,4},{6,5},{7,6},{9,8},{10,9},{11,10},{12... | collective-permute-start | bytes 9437192 | tf_op jit(solution)/shard_map/ppermute | solution.py:19
  376.1 63.9 %collective-permute-start.7 = (f32[2,3,2,1,256,256]{5,4,3,2,1,0:T(8,128)}, f32[2,3,2,1,256,256]{5,4,3,2,1,0:T(8,128)}, u32[]{:S(2)}, u32[]{:S(2)}) collective-permute-start(f32[2,3,2,1,256,256]{5,4,3,2,1,0:T(8,128)} %get-tuple-element.8), channel_id=1, source_target_pairs={{0,1},{1,2},{2,3},{3,4},{4,5},{5,6},{6,7},{8,9},{9,10},{10,11},{11... | collective-permute-start | bytes 9437192 | tf_op jit(solution)/shard_map/ppermute | solution.py:16
  474.5 11.2 %copy-start.3 = (f32[2,3,1,4,256,256]{5,4,3,2,1,0:T(8,128)S(1)}, f32[2,3,1,4,256,256]{5,4,3,2,1,0:T(8,128)}, u32[]{:S(2)}) copy-start(f32[2,3,1,4,256,256]{5,4,3,2,1,0:T(8,128)} %copy-done.2) | copy-start | bytes 18874372
  525.3 24.2 %all-to-all-start = ((f32[8,4,32,256]{3,2,1,0:T(8,128)}), f32[8,4,32,256]{3,2,1,0:T(8,128)S(1)}, u32[]{:S(2)}, u32[]{:S(2)}) async-start(f32[8,4,32,256]{3,2,1,0:T(8,128)} %fusion.56), calls=%async_computation | async-start | bytes 2097152 | tf_op jit(solution)/shard_map/all_to_all | solution.py:71
  575.1 49.5 %collective-permute-start.8 = (f32[4,256,256]{2,1,0:T(8,128)S(1)}, f32[4,256,256]{2,1,0:T(8,128)S(1)}, u32[]{:S(2)}, u32[]{:S(2)}) collective-permute-start(f32[4,256,256]{2,1,0:T(8,128)S(1)} %fusion.50), channel_id=1, source_target_pairs={{0,16},{8,24},{1,17},{9,25},{2,18},{10,26},{3,19},{11,27},{4,20},{... | collective-permute-start | bytes 3145736 | tf_op jit(solution)/shard_map/ppermute | solution.py:27
  576.4 18.2 %copy-start.10 = (u32[32]{0:T(128)S(1)}, u32[32]{0:T(128)}, u32[]{:S(2)}) copy-start(u32[32]{0:T(128)} %constant.111) | copy-start | bytes 388
  576.4 48.2 %copy-start.8 = (f32[1,4,256,256]{3,2,1,0:T(8,128)S(1)}, f32[1,4,256,256]{3,2,1,0:T(8,128)}, u32[]{:S(2)}) copy-start(f32[1,4,256,256]{3,2,1,0:T(8,128)} %param.6) | copy-start | bytes 3145732
